TPU v7x, 32 devices: a whole 2x2x4 slice. The times are simulated.
32 devices in a mesh: parts: 2 (over y), seq: 8 (over z, core), rep: 2 (over x), head: 1.
Axes of the slice: x: 2, y: 2, z: 4, core: 2. Of those that a mesh axis runs over, the one named last changes fastest.
Arguments:
- activations: bfloat16 [4, 1024, 2048], P(('parts', 'rep'), 'seq', 'head'), parts along dimension 0, may hold values from -6 to 6
- value_weight: bfloat16 [2048, 2048], P(('seq', 'rep'), 'head'), may hold values from -0.125 to 0.125
- query_in: bfloat16 [4, 1024, 2048], P(('parts', 'rep'), 'seq', 'head'), parts along dimension 0, may hold values from -6 to 6
- key_in: bfloat16 [4, 1024, 2048], P(('parts', 'rep'), 'seq', 'head'), parts along dimension 0, may hold values from -6 to 6
- grad_out: bfloat16 [4, 1024, 2048], P(('parts', 'rep'), 'seq', 'head'), parts along dimension 0, may hold values from -6 to 6
- conv_kernel: float32 [3, 4, 2048], P(None, None, 'head'), may hold values from -3 to 3
- log_gate: float32 [4, 16, 1024], P(('parts', 'rep'), 'head', 'seq'), parts along dimension 0, as said below
Outputs:
- attn_out: bfloat16 [4, 1024, 2048], P(('parts', 'rep'), 'seq', 'head'), parts along dimension 0
- grad_query: bfloat16 [4, 1024, 2048], P(('parts', 'rep'), 'seq', 'head'), parts along dimension 0
- grad_key: bfloat16 [4, 1024, 2048], P(('parts', 'rep'), 'seq', 'head'), parts along dimension 0
- grad_x: bfloat16 [4, 1024, 2048], P(('parts', 'rep'), 'seq', 'head'), parts along dimension 0
- grad_w: float32 [4096, 2048], P(('parts', 'seq', 'rep'), 'head'), parts along dimension 0
- grad_conv: float32 [6, 4, 2048], P('parts', None, 'head'), parts along dimension 0
There are 2 independent parts, one for each index of `parts`. A program takes and returns all parts, laid end to end along the dimension named above; an argument that names none is the same for every part. Nothing has to cross between parts.
Inputs may be any that keep to these rules, and one draw needn't show every extreme that they name: `log_gate`: every entry is below zero.
All inputs are finite; a program needn't handle non-finite values.
Results may differ from a plain program's by a relative error of at most 0.015.
Values may be sent and summed in bfloat16 or wider, within the bound.
A program may use at most 128 MiB of HBM per device.

v0:
```python
import math
import jax
import jax.numpy as jnp
from jax import lax
from jax.sharding import PartitionSpec as P

EPSILON = 1e-06


def shifted(block, axis, distance):
    devices = range(lax.axis_size(axis))
    route = [(i - distance, i) for i in devices if i - distance in devices]
    return lax.ppermute(block, axis, route)


def prefix(part, axis, combine, identity, reverse):
    count = lax.axis_size(axis)
    place = lax.axis_index(axis)
    ahead = count - 1 - place if reverse else place
    gathered = jax.tree.map(lambda a: lax.all_gather(a, axis), part)
    state = jax.tree.map(lambda a, e: jnp.zeros_like(a) + jnp.asarray(e, a.dtype), part, identity)

    def one(step, state):
        source = count - 1 - step if reverse else step
        return combine(
            state, jax.tree.map(lambda a: lax.dynamic_index_in_dim(a, source, 0, False), gathered)
        )

    return lax.fori_loop(0, ahead, one, state)


def carried_in(value, axis, combine, identity, reverse):
    length, mine = (lax.axis_size(axis), lax.axis_index(axis))
    everything = jax.tree.map(
        lambda part, kind: lax.all_gather(part.astype(kind), axis),
        value,
        (jnp.bfloat16, jnp.bfloat16),
    )
    start = jax.tree.map(
        lambda part, zero: jnp.broadcast_to(jnp.asarray(zero, part.dtype), part.shape),
        value,
        identity,
    )

    def step(k, before):
        at = length - 1 - k if reverse else k
        reached = at > mine if reverse else at < mine
        new = combine(
            before, jax.tree.map(lambda part, own: part[at].astype(own.dtype), everything, value)
        )
        return jax.tree.map(lambda a, b: jnp.where(reached, a, b), new, before)

    return lax.fori_loop(0, length, step, start)


def scanned(decay, state, axis, reverse):
    count = lax.axis_size(axis)
    direction = -1 if reverse else 1
    distance = 1
    while distance < count:
        far_decay, far_state = shifted((decay, state), axis, direction * distance)
        decay, state = chain_join((far_decay, far_state), (decay, state))
        distance *= 2
    return shifted(state, axis, direction)


def chain_join(earlier, following):
    return (earlier[0] * following[0], following[0][:, None, None] * earlier[1] + following[1])


def causal_filter(stream_rows, previous, kernel_taps):
    rim_rows = previous.shape[0]
    length = stream_rows.shape[0]
    extended = jnp.concatenate([previous, stream_rows], axis=0).astype(jnp.float32)
    result = jnp.zeros(stream_rows.shape, jnp.float32)
    for offset in range(kernel_taps.shape[0]):
        result = (
            result + kernel_taps[offset] * extended[rim_rows - offset : rim_rows - offset + length]
        )
    return result


def filter_back(post_rows, following_rows, kernel_taps):
    length = post_rows.shape[0]
    extended = jnp.concatenate([post_rows, following_rows], axis=0)
    result = jnp.zeros(post_rows.shape, jnp.float32)
    for offset in range(kernel_taps.shape[0]):
        result = result + kernel_taps[offset] * extended[offset : offset + length]
    return result


def tap_sums(post_rows, stream_rows, previous, kernel_width):
    rim_rows = previous.shape[0]
    length = stream_rows.shape[0]
    extended = jnp.concatenate([previous, stream_rows], axis=0).astype(jnp.float32)
    return jnp.stack(
        [
            jnp.sum(post_rows * extended[rim_rows - offset : rim_rows - offset + length], axis=0)
            for offset in range(kernel_width)
        ]
    )


def local(activations, value_weight, query_in, key_in, grad_out, conv_kernel, log_gate):
    tok_rows = query_in.shape[1]
    channels = query_in.shape[2]
    head_count = log_gate.shape[1]
    head_size = channels // head_count
    kernel_width = conv_kernel.shape[1]
    rim_rows = kernel_width - 1
    grad_scale = 1.0 / math.sqrt(lax.axis_size("seq") * lax.axis_size("rep") * tok_rows)
    query_rows = query_in[0]
    key_rows = key_in[0]
    gathered = lax.all_gather(activations, "head", axis=2, tiled=True)[0]
    columns = gathered
    value_f32 = jnp.dot(
        columns,
        lax.all_gather(value_weight, ("seq", "rep"), axis=0, tiled=True),
        preferred_element_type=jnp.float32,
    )
    value_raw = value_f32.astype(jnp.bfloat16)
    before_all = shifted(
        jnp.stack(
            [
                query_rows[tok_rows - rim_rows :],
                key_rows[tok_rows - rim_rows :],
                value_raw[tok_rows - rim_rows :],
            ]
        ),
        "seq",
        1,
    )
    before = (before_all[0], before_all[1], before_all[2])
    raw_rows = (query_rows, key_rows, value_raw)
    convolved = [
        causal_filter(raw_rows[which], before[which], conv_kernel[which]).astype(jnp.bfloat16)
        for which in range(3)
    ]
    query_heads = convolved[0].reshape(tok_rows, head_count, head_size)
    key_heads = convolved[1].reshape(tok_rows, head_count, head_size)
    value_heads = convolved[2].reshape(tok_rows, head_count, head_size)
    cumulative = jnp.cumsum(log_gate[0], axis=1)
    final_cum = cumulative[:, -1]
    block_decay = jnp.exp(final_cum)
    rising = jnp.exp(cumulative).T[:, :, None]
    shrink = jnp.exp(final_cum[:, None] - cumulative).T[:, :, None]
    mixing = jnp.exp(-jnp.abs(cumulative[:, :, None] - cumulative[:, None, :]))
    scores = (
        mixing
        * jnp.einsum("thd,shd->hts", query_heads, key_heads, preferred_element_type=jnp.float32)
    ).astype(jnp.bfloat16)
    fwd_sum = jnp.einsum(
        "thd,the->hde",
        (shrink * key_heads).astype(jnp.bfloat16),
        value_heads,
        preferred_element_type=jnp.float32,
    )
    back_sum = jnp.einsum(
        "thd,the->hde",
        (rising * key_heads).astype(jnp.bfloat16),
        value_heads,
        preferred_element_type=jnp.float32,
    )
    identity = (
        jnp.ones((head_count,), jnp.float32),
        jnp.zeros((head_count, head_size, head_size), jnp.float32),
    )
    left_b = scanned(block_decay, fwd_sum, "seq", False).astype(jnp.bfloat16)
    right_b = scanned(block_decay, back_sum, "seq", True).astype(jnp.bfloat16)
    attn = rising * jnp.einsum(
        "thd,hde->the", query_heads, left_b, preferred_element_type=jnp.float32
    )
    attn = attn + shrink * jnp.einsum(
        "thd,hde->the", query_heads, right_b, preferred_element_type=jnp.float32
    )
    attn = attn + jnp.einsum(
        "hts,she->the", scores, value_heads, preferred_element_type=jnp.float32
    )
    root_mean = jnp.sqrt(jnp.mean(attn * attn, axis=2, keepdims=True) + EPSILON)
    normed = attn / root_mean
    attn_out = normed.astype(jnp.bfloat16).reshape(1, tok_rows, channels)
    upstream = grad_out[0].reshape(tok_rows, head_count, head_size).astype(jnp.float32)
    grad_attn = (
        (upstream - normed * jnp.mean(upstream * normed, axis=2, keepdims=True)) / root_mean
    ).astype(jnp.bfloat16)
    grad_scores = (
        mixing
        * jnp.einsum("the,she->hts", grad_attn, value_heads, preferred_element_type=jnp.float32)
    ).astype(jnp.bfloat16)
    fwd_grad = jnp.einsum(
        "thd,the->hde",
        (shrink * query_heads).astype(jnp.bfloat16),
        grad_attn,
        preferred_element_type=jnp.float32,
    )
    back_grad = jnp.einsum(
        "thd,the->hde",
        (rising * query_heads).astype(jnp.bfloat16),
        grad_attn,
        preferred_element_type=jnp.float32,
    )
    left_gb = scanned(block_decay, fwd_grad, "seq", False).astype(jnp.bfloat16)
    right_gb = scanned(block_decay, back_grad, "seq", True).astype(jnp.bfloat16)
    query_post = rising * jnp.einsum(
        "the,hde->thd", grad_attn, left_b, preferred_element_type=jnp.float32
    )
    query_post = query_post + shrink * jnp.einsum(
        "the,hde->thd", grad_attn, right_b, preferred_element_type=jnp.float32
    )
    query_post = query_post + jnp.einsum(
        "hts,shd->thd", grad_scores, key_heads, preferred_element_type=jnp.float32
    )
    key_post = rising * jnp.einsum(
        "the,hde->thd", value_heads, left_gb, preferred_element_type=jnp.float32
    )
    key_post = key_post + shrink * jnp.einsum(
        "the,hde->thd", value_heads, right_gb, preferred_element_type=jnp.float32
    )
    key_post = key_post + jnp.einsum(
        "hts,thd->shd", grad_scores, query_heads, preferred_element_type=jnp.float32
    )
    value_post = rising * jnp.einsum(
        "thd,hde->the", key_heads, left_gb, preferred_element_type=jnp.float32
    )
    value_post = value_post + shrink * jnp.einsum(
        "thd,hde->the", key_heads, right_gb, preferred_element_type=jnp.float32
    )
    value_post = value_post + jnp.einsum(
        "hts,the->she", scores, grad_attn, preferred_element_type=jnp.float32
    )
    post_grads = jnp.stack(
        [
            query_post.reshape(tok_rows, channels),
            key_post.reshape(tok_rows, channels),
            value_post.reshape(tok_rows, channels),
        ]
    )
    following = shifted(post_grads[:, :rim_rows].astype(jnp.bfloat16), "seq", -1).astype(
        jnp.float32
    )
    grad_query = filter_back(post_grads[0], following[0], conv_kernel[0]).astype(jnp.bfloat16)
    grad_key = filter_back(post_grads[1], following[1], conv_kernel[1]).astype(jnp.bfloat16)
    grad_value = filter_back(post_grads[2], following[2], conv_kernel[2]).astype(jnp.bfloat16)
    kernel_terms = (
        jnp.stack(
            [
                tap_sums(post_grads[which], raw_rows[which], before[which], kernel_width)
                for which in range(3)
            ]
        )
        * grad_scale
    )
    grad_conv = lax.psum(kernel_terms, ("seq", "rep"))
    partial_x = lax.dot_general(
        grad_value,
        lax.all_gather(value_weight, ("seq", "rep"), axis=0, tiled=True),
        (((1,), (1,)), ((), ())),
        preferred_element_type=jnp.float32,
    )
    grad_x = lax.psum_scatter(
        partial_x[None].astype(jnp.bfloat16), "head", scatter_dimension=2, tiled=True
    )
    feature_rows = lax.all_to_all(gathered, ("seq", "rep"), 1, 0, tiled=True)
    grad_value_all = lax.all_gather(grad_value, ("seq", "rep"), axis=0, tiled=True)
    grad_w = (
        lax.dot_general(
            feature_rows,
            grad_value_all,
            (((0,), (0,)), ((), ())),
            preferred_element_type=jnp.float32,
        )
        * grad_scale
    )
    return (attn_out, grad_query[None], grad_key[None], grad_x, grad_w, grad_conv)


def solution(mesh):
    placed = (
        P(("parts", "rep"), "seq", "head"),
        P(("seq", "rep"), "head"),
        P(("parts", "rep"), "seq", "head"),
        P(("parts", "rep"), "seq", "head"),
        P(("parts", "rep"), "seq", "head"),
        P(None, None, "head"),
        P(("parts", "rep"), "head", "seq"),
    )
    return jax.shard_map(
        local,
        mesh=mesh,
        in_specs=placed,
        out_specs=(
            P(("parts", "rep"), "seq", "head"),
            P(("parts", "rep"), "seq", "head"),
            P(("parts", "rep"), "seq", "head"),
            P(("parts", "rep"), "seq", "head"),
            P(("parts", "seq", "rep"), "head"),
            P("parts", None, "head"),
        ),
        check_vma=False,
    )
```

profile of v0, /device:TPU:0, one launch (start us, length us, event | category | flops | bytes accessed | tf_op | source)
XLA Modules:
  0.0 546.2 jit_solution(14763116871213756074)
XLA Ops:
  11.9 75.3 %all-gather.3.cloned.1.call-done = bf16[2048,2048]{1,0:T(8,128)(2,1)} async-done(((bf16[128,2048]{1,0:T(8,128)(2,1)}), bf16[2048,2048]{1,0:T(8,128)(2,1)}) %all-gather.3.cloned.1.call-update) | async-done | bytes 8388624 | tf_op jit(solution)/shard_map/all_gather | solution.py:118
  87.2 4.6 convolution_convert_fusion.1
  92.0 2.2 collective-permute-start.2
  99.4 3.4 collective-permute-start.3
  103.1 1.3 collective-permute-start.9
  105.0 4.4 collective-permute-done.9
  109.9 1.3 collective-permute-start.10
  111.2 14.4 %collective-permute-start.4 = (f32[16,128,128]{2,1,0:T(8,128)S(1)}, f32[16,128,128]{2,1,0:T(8,128)S(1)}, u32[]{:S(2)}, u32[]{:S(2)}) collective-permute-start(f32[16,128,128]{2,1,0:T(8,128)S(1)} %get-tuple-element.65), channel_id=1, source_target_pairs={{0,4},{2,6},{4,8},{6,10},{8,12},{10,14},{1,5},{3,7},{5,9},{7,11},{... | collective-permute-start | bytes 3145736 | tf_op jit(solution)/shard_map/ppermute | solution.py:13
  125.6 3.6 collective-permute-start
  129.3 1.3 collective-permute-start.7
  130.6 1.7 collective-permute-done.7
  132.3 14.0 %collective-permute-done.10 = f32[16,128,128]{2,1,0:T(8,128)S(1)} collective-permute-done((f32[16,128,128]{2,1,0:T(8,128)S(1)}, f32[16,128,128]{2,1,0:T(8,128)S(1)}, u32[]{:S(2)}, u32[]{:S(2)}) %collective-permute-start.10) | collective-permute-done | bytes 1048608 | tf_op jit(solution)/shard_map/ppermute | solution.py:13
  150.0 10.6 %collective-permute-start.5 = (f32[16,128,128]{2,1,0:T(8,128)}, f32[16,128,128]{2,1,0:T(8,128)}, u32[]{:S(2)}, u32[]{:S(2)}) collective-permute-start(f32[16,128,128]{2,1,0:T(8,128)} %multiply_add_fusion.10), channel_id=1, source_target_pairs={{0,8},{2,10},{4,12},{6,14},{1,9},{3,11},{5,13},{7,15},{16,24},{18,... | collective-permute-start | bytes 3145736 | tf_op jit(solution)/shard_map/ppermute | solution.py:13
  160.6 2.2 copy.108
  162.8 4.0 collective-permute-start.1
  166.8 1.3 collective-permute-start.8
  168.1 13.9 %collective-permute-done.1 = f32[16]{0:T(128)S(1)} collective-permute-done((f32[16]{0:T(128)S(1)}, f32[16]{0:T(128)S(1)}, u32[]{:S(2)}, u32[]{:S(2)}) %collective-permute-start.1) | collective-permute-done | bytes 96 | tf_op jit(solution)/shard_map/ppermute | solution.py:13
  183.3 2.0 copy.99
  185.3 1.7 fusion.18
  187.1 14.1 %collective-permute-done.11 = f32[16,128,128]{2,1,0:T(8,128)} collective-permute-done((f32[16,128,128]{2,1,0:T(8,128)}, f32[16,128,128]{2,1,0:T(8,128)}, u32[]{:S(2)}, u32[]{:S(2)}) %collective-permute-start.11) | collective-permute-done | bytes 1048608 | tf_op jit(solution)/shard_map/ppermute | solution.py:13
  201.2 1.7 multiply_add_fusion.6
  202.9 1.4 collective-permute-start.12
  204.3 1.7 multiply_add_fusion.9
  206.1 3.2 collective-permute-start.6
  213.6 16.0 %collective-permute-start.13 = (f32[16,128,128]{2,1,0:T(8,128)S(1)}, f32[16,128,128]{2,1,0:T(8,128)S(1)}, u32[]{:S(2)}, u32[]{:S(2)}) collective-permute-start(f32[16,128,128]{2,1,0:T(8,128)S(1)} %fusion.53), channel_id=1, source_target_pairs={{0,2},{2,4},{4,6},{6,8},{8,10},{10,12},{12,14},{1,3},{3,5},{5,7},{... | collective-permute-start | bytes 3145736 | tf_op jit(solution)/shard_map/ppermute | solution.py:13
  229.6 1.3 collective-permute-start.17
  231.8 4.3 collective-permute-done.17
  236.7 1.3 collective-permute-start.18
  238.0 14.6 %collective-permute-start.14 = (f32[16,128,128]{2,1,0:T(8,128)S(1)}, f32[16,128,128]{2,1,0:T(8,128)S(1)}, u32[]{:S(2)}, u32[]{:S(2)}) collective-permute-start(f32[16,128,128]{2,1,0:T(8,128)S(1)} %get-tuple-element.61), channel_id=1, source_target_pairs={{0,4},{2,6},{4,8},{6,10},{8,12},{10,14},{1,5},{3,7},{5,9},{7,11},{... | collective-permute-start | bytes 3145736 | tf_op jit(solution)/shard_map/ppermute | solution.py:13
  253.4 19.0 %collective-permute-done.18 = f32[16,128,128]{2,1,0:T(8,128)S(1)} collective-permute-done((f32[16,128,128]{2,1,0:T(8,128)S(1)}, f32[16,128,128]{2,1,0:T(8,128)S(1)}, u32[]{:S(2)}, u32[]{:S(2)}) %collective-permute-start.18) | collective-permute-done | bytes 1048608 | tf_op jit(solution)/shard_map/ppermute | solution.py:13
  273.6 1.4 collective-permute-start.19
  276.2 9.0 %collective-permute-start.15 = (f32[16,128,128]{2,1,0:T(8,128)}, f32[16,128,128]{2,1,0:T(8,128)}, u32[]{:S(2)}, u32[]{:S(2)}) collective-permute-start(f32[16,128,128]{2,1,0:T(8,128)} %multiply_add_fusion.4), channel_id=1, source_target_pairs={{0,8},{2,10},{4,12},{6,14},{1,9},{3,11},{5,13},{7,15},{16,24},{18,... | collective-permute-start | bytes 3145736 | tf_op jit(solution)/shard_map/ppermute | solution.py:13
  285.7 1.5 fusion.91
  287.2 2.0 copy.156
  289.3 1.5 convolution_bitcast_fusion.3
  290.8 36.1 %collective-permute-done.19 = f32[16,128,128]{2,1,0:T(8,128)} collective-permute-done((f32[16,128,128]{2,1,0:T(8,128)}, f32[16,128,128]{2,1,0:T(8,128)}, u32[]{:S(2)}, u32[]{:S(2)}) %collective-permute-start.19) | collective-permute-done | bytes 1048608 | tf_op jit(solution)/shard_map/ppermute | solution.py:13
  326.9 1.7 multiply_add_fusion
  328.6 1.4 collective-permute-start.20
  330.1 1.7 multiply_add_fusion.3
  331.8 3.2 collective-permute-start.16
  335.1 1.4 convolution_bitcast_fusion
  336.9 1.7 fusion.90
  338.6 2.0 copy.157
  340.6 1.7 fusion.2
  342.5 1.5 fusion.89
  344.0 2.0 copy.158
  346.8 1.3 collective-permute-start.21
  348.1 2.6 copy.159
  350.7 4.3 collective-permute-done.21
  355.0 4.4 multiply_reduce_fusion.3
  359.5 2.0 copy.129
  361.5 29.8 %all_to_all.19 = bf16[128,16,128]{0,2,1:T(8,128)(2,1)} all-to-all(bf16[128,16,128]{0,2,1:T(8,128)(2,1)} %bitcast.200), channel_id=1, replica_groups=mesh['parts'=2,'seq'=8,'rep'=2,'head'=1] {'seq','rep'}, dimensions={1} | all-to-all | bytes 1048576 | tf_op jit(solution)/shard_map/all_to_all | solution.py:263
  391.3 2.0 copy.130
  393.4 1.3 copy.113
  394.7 2.1 copy.139
  396.8 1.3 copy.126
  398.2 4.1 multiply_reduce_fusion.11
  402.4 1.7 multiply_reduce_fusion.7
  404.9 8.2 %fusion.1 = bf16[1,128,2048]{2,1,0:T(8,128)(2,1)} fusion(bf16[128,2048]{1,0:T(8,128)(2,1)S(1)} %copy-done.10, bf16[2048,2048]{1,0:T(8,128)(2,1)} %all-gather.3.cloned.1.call-done), kind=kOutput, calls=%fused_computation.4 | convolution fusion | flops 1074003968 | bytes 9437184 | tf_op jit(solution)/shard_map/dot_general | solution.py:254
  413.1 33.6 %all-gather.5.cloned.1.call-done = bf16[2048,2048]{1,0:T(8,128)(2,1)} async-done(((bf16[128,2048]{1,0:T(8,128)(2,1)}), bf16[2048,2048]{1,0:T(8,128)(2,1)}) %all-gather.5.cloned.1.call-update) | async-done | bytes 8388624 | tf_op jit(solution)/shard_map/all_gather | solution.py:264
  446.7 5.8 %fusion = f32[128,2048]{0,1:T(8,128)S(1)} fusion(bf16[2048,2048]{1,0:T(8,128)(2,1)} %all-gather.5.cloned.1.call-done, bf16[2048,128]{1,0:T(8,128)(2,1)S(1)} %bitcast.204), kind=kOutput, calls=%fused_computation.1 | convolution fusion | flops 1074003968 | bytes 9961472 | tf_op jit(solution)/shard_map/dot_general | solution.py:266
  452.5 1.3 copy.140
  453.8 84.3 %all-reduce.2.cloned.1.call-done = f32[3,4,2048]{2,1,0:T(4,128)} async-done(((f32[3,4,2048]{2,1,0:T(4,128)}), f32[3,4,2048]{2,1,0:T(4,128)}) %all-reduce.2.cloned.1.call-update) | async-done | bytes 98320 | tf_op jit(solution)/shard_map/psum | solution.py:253
  538.1 1.5 copy.188
  (119 shorter events, 28.1 us)
Async XLA Ops:
  7.2 80.1 %copy-start.15 = (bf16[1,128,2048]{2,1,0:T(8,128)(2,1)S(1)}, bf16[1,128,2048]{2,1,0:T(8,128)(2,1)}, u32[]{:S(2)}) copy-start(bf16[1,128,2048]{2,1,0:T(8,128)(2,1)} %param.7) | copy-start | bytes 1572868
  7.2 80.1 %all-gather.3.cloned.1.call-start = ((), (), s32[]{:S(2)}) async-start(), calls=%async_computation.1 | async-start | bytes 8912896 | tf_op jit(solution)/shard_map/all_gather | solution.py:118
  7.9 438.8 %all-gather.5.cloned.1.call-start = ((), (), s32[]{:S(2)}) async-start(), calls=%async_computation.2 | async-start | bytes 8912896 | tf_op jit(solution)/shard_map/all_gather | solution.py:264
  11.9 83.2 %copy-start.23 = (bf16[1,128,2048]{2,1,0:T(8,128)(2,1)S(1)}, bf16[1,128,2048]{2,1,0:T(8,128)(2,1)}, u32[]{:S(2)}) copy-start(bf16[1,128,2048]{2,1,0:T(8,128)(2,1)} %param.10) | copy-start | bytes 1572868
  11.9 83.2 %copy-start.24 = (bf16[1,128,2048]{2,1,0:T(8,128)(2,1)S(1)}, bf16[1,128,2048]{2,1,0:T(8,128)(2,1)}, u32[]{:S(2)}) copy-start(bf16[1,128,2048]{2,1,0:T(8,128)(2,1)} %param.9) | copy-start | bytes 1572868
  91.9 3.1 copy-start.16
  92.0 3.0 collective-permute-start.2
  98.0 1.0 copy-start.3
  98.5 4.5 copy-start
  99.4 5.6 %collective-permute-start.3 = (f32[16,128,128]{2,1,0:T(8,128)S(1)}, f32[16,128,128]{2,1,0:T(8,128)S(1)}, u32[]{:S(2)}, u32[]{:S(2)}) collective-permute-start(f32[16,128,128]{2,1,0:T(8,128)S(1)} %fusion.57), channel_id=1, source_target_pairs={{0,2},{2,4},{4,6},{6,8},{8,10},{10,12},{12,14},{1,3},{3,5},{5,7},{... | collective-permute-start | bytes 3145736 | tf_op jit(solution)/shard_map/ppermute | solution.py:13
  103.1 6.3 %collective-permute-start.9 = (f32[16,128,128]{2,1,0:T(8,128)S(1)}, f32[16,128,128]{2,1,0:T(8,128)S(1)}, u32[]{:S(2)}, u32[]{:S(2)}) collective-permute-start(f32[16,128,128]{2,1,0:T(8,128)S(1)} %fusion.55), channel_id=1, source_target_pairs={{2,0},{4,2},{6,4},{8,6},{10,8},{12,10},{14,12},{3,1},{5,3},{7,5},{... | collective-permute-start | bytes 3145736 | tf_op jit(solution)/shard_map/ppermute | solution.py:13
  109.9 36.4 %collective-permute-start.10 = (f32[16,128,128]{2,1,0:T(8,128)S(1)}, f32[16,128,128]{2,1,0:T(8,128)S(1)}, u32[]{:S(2)}, u32[]{:S(2)}) collective-permute-start(f32[16,128,128]{2,1,0:T(8,128)S(1)} %get-tuple-element.66), channel_id=1, source_target_pairs={{4,0},{6,2},{8,4},{10,6},{12,8},{14,10},{5,1},{7,3},{9,5},{11,7},{... | collective-permute-start | bytes 3145736 | tf_op jit(solution)/shard_map/ppermute | solution.py:13
  111.2 37.6 %collective-permute-start.4 = (f32[16,128,128]{2,1,0:T(8,128)S(1)}, f32[16,128,128]{2,1,0:T(8,128)S(1)}, u32[]{:S(2)}, u32[]{:S(2)}) collective-permute-start(f32[16,128,128]{2,1,0:T(8,128)S(1)} %get-tuple-element.65), channel_id=1, source_target_pairs={{0,4},{2,6},{4,8},{6,10},{8,12},{10,14},{1,5},{3,7},{5,9},{7,11},{... | collective-permute-start | bytes 3145736 | tf_op jit(solution)/shard_map/ppermute | solution.py:13
  125.6 4.9 collective-permute-start
  129.3 3.1 collective-permute-start.7
  147.6 53.6 %collective-permute-start.11 = (f32[16,128,128]{2,1,0:T(8,128)}, f32[16,128,128]{2,1,0:T(8,128)}, u32[]{:S(2)}, u32[]{:S(2)}) collective-permute-start(f32[16,128,128]{2,1,0:T(8,128)} %multiply_add_fusion.7), channel_id=1, source_target_pairs={{8,0},{10,2},{12,4},{14,6},{9,1},{11,3},{13,5},{15,7},{24,16},{26,... | collective-permute-start | bytes 3145736 | tf_op jit(solution)/shard_map/ppermute | solution.py:13
  150.0 54.3 %collective-permute-start.5 = (f32[16,128,128]{2,1,0:T(8,128)}, f32[16,128,128]{2,1,0:T(8,128)}, u32[]{:S(2)}, u32[]{:S(2)}) collective-permute-start(f32[16,128,128]{2,1,0:T(8,128)} %multiply_add_fusion.10), channel_id=1, source_target_pairs={{0,8},{2,10},{4,12},{6,14},{1,9},{3,11},{5,13},{7,15},{16,24},{18,... | collective-permute-start | bytes 3145736 | tf_op jit(solution)/shard_map/ppermute | solution.py:13
  162.8 19.2 %collective-permute-start.1 = (f32[16]{0:T(128)S(1)}, f32[16]{0:T(128)S(1)}, u32[]{:S(2)}, u32[]{:S(2)}) collective-permute-start(f32[16]{0:T(128)S(1)} %get-tuple-element.63), channel_id=1, source_target_pairs={{0,4},{2,6},{4,8},{6,10},{8,12},{10,14},{1,5},{3,7},{5,9},{7,11},{... | collective-permute-start | bytes 200 | tf_op jit(solution)/shard_map/ppermute | solution.py:13
  166.8 15.2 %collective-permute-start.8 = (f32[16]{0:T(128)S(1)}, f32[16]{0:T(128)S(1)}, u32[]{:S(2)}, u32[]{:S(2)}) collective-permute-start(f32[16]{0:T(128)S(1)} %get-tuple-element.64), channel_id=1, source_target_pairs={{4,0},{6,2},{8,4},{10,6},{12,8},{14,10},{5,1},{7,3},{9,5},{11,7},{... | collective-permute-start | bytes 200 | tf_op jit(solution)/shard_map/ppermute | solution.py:13
  187.1 22.2 %copy-start.19 = (bf16[16,128,128]{2,1,0:T(8,128)(2,1)}, bf16[16,128,128]{2,1,0:T(8,128)(2,1)S(1)}, u32[]{:S(2)}) copy-start(bf16[16,128,128]{2,1,0:T(8,128)(2,1)S(1)} %fusion.18) | copy-start | bytes 1572868
  202.9 6.4 %copy-start.1 = (bf16[16,16,8,128]{3,2,1,0:T(8,128)(2,1)S(1)}, bf16[16,16,8,128]{3,2,1,0:T(8,128)(2,1)}, u32[]{:S(2)}) copy-start(bf16[16,16,8,128]{3,2,1,0:T(8,128)(2,1)} %copy-done) | copy-start | bytes 1572868
  202.9 6.9 %collective-permute-start.12 = (bf16[16,128,128]{2,1,0:T(8,128)(2,1)S(1)}, bf16[16,128,128]{2,1,0:T(8,128)(2,1)S(1)}, u32[]{:S(2)}, u32[]{:S(2)}) collective-permute-start(bf16[16,128,128]{2,1,0:T(8,128)(2,1)S(1)} %multiply_add_fusion.6), channel_id=1, source_target_pairs={{2,0},{4,2},{6,4},{8,6},{10,8},{12,10},{14,12},{3,1},{5,3},{7,5},{... | collective-permute-start | bytes 1572872 | tf_op jit(solution)/shard_map/ppermute | solution.py:13
  206.1 3.8 copy-start.8
  206.1 4.7 collective-permute-start.6
  210.2 1.2 copy-start.9
  212.6 73.1 %copy-start.6 = (bf16[128,16,128]{0,2,1:T(8,128)(2,1)}, bf16[128,16,128]{0,2,1:T(8,128)(2,1)S(1)}, u32[]{:S(2)}) copy-start(bf16[128,16,128]{0,2,1:T(8,128)(2,1)S(1)} %get-tuple-element.36) | copy-start | bytes 1572868
  213.6 18.2 %collective-permute-start.13 = (f32[16,128,128]{2,1,0:T(8,128)S(1)}, f32[16,128,128]{2,1,0:T(8,128)S(1)}, u32[]{:S(2)}, u32[]{:S(2)}) collective-permute-start(f32[16,128,128]{2,1,0:T(8,128)S(1)} %fusion.53), channel_id=1, source_target_pairs={{0,2},{2,4},{4,6},{6,8},{8,10},{10,12},{12,14},{1,3},{3,5},{5,7},{... | collective-permute-start | bytes 3145736 | tf_op jit(solution)/shard_map/ppermute | solution.py:13
  229.6 6.5 %collective-permute-start.17 = (f32[16,128,128]{2,1,0:T(8,128)S(1)}, f32[16,128,128]{2,1,0:T(8,128)S(1)}, u32[]{:S(2)}, u32[]{:S(2)}) collective-permute-start(f32[16,128,128]{2,1,0:T(8,128)S(1)} %fusion.51), channel_id=1, source_target_pairs={{2,0},{4,2},{6,4},{8,6},{10,8},{12,10},{14,12},{3,1},{5,3},{7,5},{... | collective-permute-start | bytes 3145736 | tf_op jit(solution)/shard_map/ppermute | solution.py:13
  236.7 35.7 %collective-permute-start.18 = (f32[16,128,128]{2,1,0:T(8,128)S(1)}, f32[16,128,128]{2,1,0:T(8,128)S(1)}, u32[]{:S(2)}, u32[]{:S(2)}) collective-permute-start(f32[16,128,128]{2,1,0:T(8,128)S(1)} %get-tuple-element.62), channel_id=1, source_target_pairs={{4,0},{6,2},{8,4},{10,6},{12,8},{14,10},{5,1},{7,3},{9,5},{11,7},{... | collective-permute-start | bytes 3145736 | tf_op jit(solution)/shard_map/ppermute | solution.py:13
  238.0 37.1 %collective-permute-start.14 = (f32[16,128,128]{2,1,0:T(8,128)S(1)}, f32[16,128,128]{2,1,0:T(8,128)S(1)}, u32[]{:S(2)}, u32[]{:S(2)}) collective-permute-start(f32[16,128,128]{2,1,0:T(8,128)S(1)} %get-tuple-element.61), channel_id=1, source_target_pairs={{0,4},{2,6},{4,8},{6,10},{8,12},{10,14},{1,5},{3,7},{5,9},{7,11},{... | collective-permute-start | bytes 3145736 | tf_op jit(solution)/shard_map/ppermute | solution.py:13
  253.1 32.1 %copy-start.21 = (bf16[16,128,128]{2,1,0:T(8,128)(2,1)}, bf16[16,128,128]{2,1,0:T(8,128)(2,1)S(1)}, u32[]{:S(2)}) copy-start(bf16[16,128,128]{2,1,0:T(8,128)(2,1)S(1)} %fusion.19) | copy-start | bytes 1572868
  273.6 11.6 %copy-start.4 = (bf16[128,2048]{0,1:T(8,128)(2,1)S(1)}, bf16[128,2048]{0,1:T(8,128)(2,1)}, u32[]{:S(2)}) copy-start(bf16[128,2048]{0,1:T(8,128)(2,1)} %copy.97) | copy-start | bytes 1572868
  273.6 53.3 %collective-permute-start.19 = (f32[16,128,128]{2,1,0:T(8,128)}, f32[16,128,128]{2,1,0:T(8,128)}, u32[]{:S(2)}, u32[]{:S(2)}) collective-permute-start(f32[16,128,128]{2,1,0:T(8,128)} %multiply_add_fusion.1), channel_id=1, source_target_pairs={{8,0},{10,2},{12,4},{14,6},{9,1},{11,3},{13,5},{15,7},{24,16},{26,... | collective-permute-start | bytes 3145736 | tf_op jit(solution)/shard_map/ppermute | solution.py:13
  276.2 53.9 %collective-permute-start.15 = (f32[16,128,128]{2,1,0:T(8,128)}, f32[16,128,128]{2,1,0:T(8,128)}, u32[]{:S(2)}, u32[]{:S(2)}) collective-permute-start(f32[16,128,128]{2,1,0:T(8,128)} %multiply_add_fusion.4), channel_id=1, source_target_pairs={{0,8},{2,10},{4,12},{6,14},{1,9},{3,11},{5,13},{7,15},{16,24},{18,... | collective-permute-start | bytes 3145736 | tf_op jit(solution)/shard_map/ppermute | solution.py:13
  328.6 6.4 %copy-start.7 = (bf16[128,16,128]{0,2,1:T(8,128)(2,1)S(1)}, bf16[128,16,128]{0,2,1:T(8,128)(2,1)}, u32[]{:S(2)}) copy-start(bf16[128,16,128]{0,2,1:T(8,128)(2,1)} %copy-done.6) | copy-start | bytes 1572868
  328.6 6.4 %copy-start.20 = (bf16[16,128,128]{2,1,0:T(8,128)(2,1)S(1)}, bf16[16,128,128]{2,1,0:T(8,128)(2,1)}, u32[]{:S(2)}) copy-start(bf16[16,128,128]{2,1,0:T(8,128)(2,1)} %copy-done.19) | copy-start | bytes 1572868
  328.6 7.8 %collective-permute-start.20 = (bf16[16,128,128]{2,1,0:T(8,128)(2,1)S(1)}, bf16[16,128,128]{2,1,0:T(8,128)(2,1)S(1)}, u32[]{:S(2)}, u32[]{:S(2)}) collective-permute-start(bf16[16,128,128]{2,1,0:T(8,128)(2,1)S(1)} %multiply_add_fusion), channel_id=1, source_target_pairs={{2,0},{4,2},{6,4},{8,6},{10,8},{12,10},{14,12},{3,1},{5,3},{7,5},{... | collective-permute-start | bytes 1572872 | tf_op jit(solution)/shard_map/ppermute | solution.py:13
  331.8 4.6 copy-start.2
  331.8 5.1 collective-permute-start.16
  336.4 2.2 copy-start.22
  336.9 1.7 copy-start.17
  340.6 1.7 copy-start.5
  340.6 1.7 copy-start.14
  340.6 1.8 copy-start.18
  346.8 8.2 %collective-permute-start.21 = (bf16[3,3,2048]{2,1,0:T(4,128)(2,1)S(1)}, bf16[3,3,2048]{2,1,0:T(4,128)(2,1)S(1)}, u32[]{:S(2)}, u32[]{:S(2)}) collective-permute-start(bf16[3,3,2048]{2,1,0:T(4,128)(2,1)S(1)} %pad_maximum_fusion.3), channel_id=1, source_target_pairs={{2,0},{4,2},{6,4},{8,6},{10,8},{12,10},{14,12},{3,1},{5,3},{7,5},{... | collective-permute-start | bytes 110600 | tf_op jit(solution)/shard_map/ppermute | solution.py:13
  359.4 178.6 %all-reduce.2.cloned.1.call-start = ((), (), s32[]{:S(2)}) async-start(), calls=%async_computation.3 | async-start | bytes 196608 | tf_op jit(solution)/shard_map/psum | solution.py:253
  361.5 31.9 %copy-start.11 = (f32[128,16,128]{0,2,1:T(8,128)S(1)}, f32[128,16,128]{0,2,1:T(8,128)}, u32[]{:S(2)}) copy-start(f32[128,16,128]{0,2,1:T(8,128)} %get-tuple-element.74) | copy-start | bytes 3145732
  394.7 2.1 copy-start.12
  398.2 4.2 copy-start.13
  402.4 2.5 copy-start.10
  404.9 41.8 %copy-start.25 = (bf16[16,128,128]{2,1,0:T(8,128)(2,1)S(1)}, bf16[16,128,128]{2,1,0:T(8,128)(2,1)}, u32[]{:S(2)}) copy-start(bf16[16,128,128]{2,1,0:T(8,128)(2,1)} %copy.130) | copy-start | bytes 1572868
Sparse Core Ops, SparseCore 0:
  10.2 76.9 all-gather.2
  359.6 87.0 all-gather.4
  450.7 87.3 all-reduce.1
where the time goes:
time: 548 us; the launch traced here: 546 us
  waiting for transfers between devices  309 us (56%)
  starting transfers between devices  98.8 us (18%)
  matrix products  34.2 us (6%)
  other arithmetic  30.6 us (6%)
  blocking collectives  29.8 us (5%)
  local copies, waits for them, and re-layouts  29.6 us (5%)
  between operations  14.4 us (3%)
    ppermute x22, waiting for transfers between devices, shifted(): return lax.ppermute(block, axis, route)  115 us
    ppermute x22, starting transfers between devices, shifted(): return lax.ppermute(block, axis, route)  98.7 us
    psum x1, waiting for transfers between devices, local(): grad_conv = lax.psum(kernel_terms, ('seq', 'rep'))  84.3 us
    all_gather x1, waiting for transfers between devices, local(): lax.all_gather(value_weight, ('seq', 'rep'), axis=0, tiled=True)  75.3 us
    all_gather x1, waiting for transfers between devices, local(): lax.all_gather(grad_value, ('seq', 'rep'), axis=0, tiled=True)  33.6 us
    all_to_all x1, blocking collectives, local(): feature_rows = lax.all_to_all(gathered, ('seq', 'rep'), 1, 0, tiled=True)  29.8 us
    add x10, other arithmetic, chain_join(): following[0][:, None, None] * earlier[1] + following[1]  12.7 us
  transfers between devices with their start and end apart: 25, of which 16 were waited for; matrix products, arithmetic and copies ran while one was open for 12% of the time, Pallas kernels for 0%

commit v1 on v0

--- a/solution.py
+++ b/solution.py
@@ -250,7 +250,7 @@
         )
         * grad_scale
     )
-    grad_conv = lax.psum(kernel_terms, ("seq", "rep"))
+    grad_conv = jax.lax.all_gather(kernel_terms, ("seq", "rep")).sum(axis=0)
     partial_x = lax.dot_general(
         grad_value,
         lax.all_gather(value_weight, ("seq", "rep"), axis=0, tiled=True),

time: 548 us -> 505 us (0.922)
  waiting for transfers between devices: 309 us -> 271 us
    psum x1 -> x0, waiting for transfers between devices: 84.3 us -> none  [local(): grad_conv = lax.psum(kernel_terms, ('seq', 'rep'))]
    all_gather x1, waiting for transfers between devices: 33.6 us -> 73.5 us  [local(): lax.all_gather(grad_value, ('seq', 'rep'), axis=0, tiled=True)]
    all_gather x0 -> x1, waiting for transfers between devices: none -> 10 us  [local(): grad_conv = jax.lax.all_gather(kernel_terms, ('seq', 'rep')).sum(axis=0)]
  transfers between devices with their start and end apart: 25 -> 25, of which waited for: 16 -> 15; matrix products, arithmetic and copies ran while one was open for 12% -> 10% of each run, Pallas kernels for 0% -> 0%
where the time goes in v1:
time: 505 us; the launch traced here: 503 us
  waiting for transfers between devices  271 us (54%)
  starting transfers between devices  98.8 us (20%)
  matrix products  33.2 us (7%)
  other arithmetic  30.5 us (6%)
  blocking collectives  29.9 us (6%)
  local copies, waits for them, and re-layouts  25.8 us (5%)
  between operations  14.5 us (3%)
    ppermute x22, waiting for transfers between devices, shifted(): return lax.ppermute(block, axis, route)  110 us
    ppermute x22, starting transfers between devices, shifted(): return lax.ppermute(block, axis, route)  98.7 us
    all_gather x1, waiting for transfers between devices, local(): lax.all_gather(value_weight, ('seq', 'rep'), axis=0, tiled=True)  75.4 us
    all_gather x1, waiting for transfers between devices, local(): lax.all_gather(grad_value, ('seq', 'rep'), axis=0, tiled=True)  73.5 us
    all_to_all x1, blocking collectives, local(): feature_rows = lax.all_to_all(gathered, ('seq', 'rep'), 1, 0, tiled=True)  29.9 us
    add x10, other arithmetic, chain_join(): following[0][:, None, None] * earlier[1] + following[1]  12.7 us
  transfers between devices with their start and end apart: 25, of which 15 were waited for; matrix products, arithmetic and copies ran while one was open for 10% of the time, Pallas kernels for 0%

profile of v1, /device:TPU:0, one launch (start us, length us, event | category | flops | bytes accessed | tf_op | source)
XLA Modules:
  0.0 503.4 jit_solution(15200036045377254061)
XLA Ops:
  11.8 75.4 %all-gather.4.cloned.1.call-done = bf16[2048,2048]{1,0:T(8,128)(2,1)} async-done(((bf16[128,2048]{1,0:T(8,128)(2,1)}), bf16[2048,2048]{1,0:T(8,128)(2,1)}) %all-gather.4.cloned.1.call-update) | async-done | bytes 8388624 | tf_op jit(solution)/shard_map/all_gather | solution.py:118
  87.2 4.6 convolution_convert_fusion.1
  92.0 2.2 collective-permute-start.2
  99.4 3.4 collective-permute-start.3
  103.1 1.3 collective-permute-start.9
  105.0 4.4 collective-permute-done.9
  109.9 1.3 collective-permute-start.10
  111.2 14.4 %collective-permute-start.4 = (f32[16,128,128]{2,1,0:T(8,128)S(1)}, f32[16,128,128]{2,1,0:T(8,128)S(1)}, u32[]{:S(2)}, u32[]{:S(2)}) collective-permute-start(f32[16,128,128]{2,1,0:T(8,128)S(1)} %get-tuple-element.71), channel_id=1, source_target_pairs={{0,4},{2,6},{4,8},{6,10},{8,12},{10,14},{1,5},{3,7},{5,9},{7,11},{... | collective-permute-start | bytes 3145736 | tf_op jit(solution)/shard_map/ppermute | solution.py:13
  125.6 3.6 collective-permute-start
  129.3 1.3 collective-permute-start.7
  130.6 1.7 collective-permute-done.7
  132.3 14.0 %collective-permute-done.10 = f32[16,128,128]{2,1,0:T(8,128)S(1)} collective-permute-done((f32[16,128,128]{2,1,0:T(8,128)S(1)}, f32[16,128,128]{2,1,0:T(8,128)S(1)}, u32[]{:S(2)}, u32[]{:S(2)}) %collective-permute-start.10) | collective-permute-done | bytes 1048608 | tf_op jit(solution)/shard_map/ppermute | solution.py:13
  146.3 1.2 multiply_add_fusion.7
  147.5 1.3 collective-permute-start.11
  150.0 10.6 %collective-permute-start.5 = (f32[16,128,128]{2,1,0:T(8,128)}, f32[16,128,128]{2,1,0:T(8,128)}, u32[]{:S(2)}, u32[]{:S(2)}) collective-permute-start(f32[16,128,128]{2,1,0:T(8,128)} %multiply_add_fusion.10), channel_id=1, source_target_pairs={{0,8},{2,10},{4,12},{6,14},{1,9},{3,11},{5,13},{7,15},{16,24},{18,... | collective-permute-start | bytes 3145736 | tf_op jit(solution)/shard_map/ppermute | solution.py:13
  160.6 2.2 copy.152
  162.8 4.0 collective-permute-start.1
  166.8 1.3 collective-permute-start.8
  168.1 13.9 %collective-permute-done.1 = f32[16]{0:T(128)S(1)} collective-permute-done((f32[16]{0:T(128)S(1)}, f32[16]{0:T(128)S(1)}, u32[]{:S(2)}, u32[]{:S(2)}) %collective-permute-start.1) | collective-permute-done | bytes 96 | tf_op jit(solution)/shard_map/ppermute | solution.py:13
  182.0 1.3 add_convert_fusion
  183.3 2.0 copy.143
  185.3 1.7 fusion.18
  187.1 14.1 %collective-permute-done.11 = f32[16,128,128]{2,1,0:T(8,128)} collective-permute-done((f32[16,128,128]{2,1,0:T(8,128)}, f32[16,128,128]{2,1,0:T(8,128)}, u32[]{:S(2)}, u32[]{:S(2)}) %collective-permute-start.11) | collective-permute-done | bytes 1048608 | tf_op jit(solution)/shard_map/ppermute | solution.py:13
  201.1 1.7 multiply_add_fusion.6
  202.9 1.4 collective-permute-start.12
  204.3 1.7 multiply_add_fusion.9
  206.1 3.2 collective-permute-start.6
  213.6 16.0 %collective-permute-start.13 = (f32[16,128,128]{2,1,0:T(8,128)S(1)}, f32[16,128,128]{2,1,0:T(8,128)S(1)}, u32[]{:S(2)}, u32[]{:S(2)}) collective-permute-start(f32[16,128,128]{2,1,0:T(8,128)S(1)} %fusion.53), channel_id=1, source_target_pairs={{0,2},{2,4},{4,6},{6,8},{8,10},{10,12},{12,14},{1,3},{3,5},{5,7},{... | collective-permute-start | bytes 3145736 | tf_op jit(solution)/shard_map/ppermute | solution.py:13
  229.6 1.3 collective-permute-start.17
  231.8 4.3 collective-permute-done.17
  236.7 1.3 collective-permute-start.18
  238.0 14.6 %collective-permute-start.14 = (f32[16,128,128]{2,1,0:T(8,128)S(1)}, f32[16,128,128]{2,1,0:T(8,128)S(1)}, u32[]{:S(2)}, u32[]{:S(2)}) collective-permute-start(f32[16,128,128]{2,1,0:T(8,128)S(1)} %get-tuple-element.67), channel_id=1, source_target_pairs={{0,4},{2,6},{4,8},{6,10},{8,12},{10,14},{1,5},{3,7},{5,9},{7,11},{... | collective-permute-start | bytes 3145736 | tf_op jit(solution)/shard_map/ppermute | solution.py:13
  253.4 19.0 %collective-permute-done.18 = f32[16,128,128]{2,1,0:T(8,128)S(1)} collective-permute-done((f32[16,128,128]{2,1,0:T(8,128)S(1)}, f32[16,128,128]{2,1,0:T(8,128)S(1)}, u32[]{:S(2)}, u32[]{:S(2)}) %collective-permute-start.18) | collective-permute-done | bytes 1048608 | tf_op jit(solution)/shard_map/ppermute | solution.py:13
  272.4 1.2 multiply_add_fusion.1
  273.6 1.4 collective-permute-start.19
  276.2 9.0 %collective-permute-start.15 = (f32[16,128,128]{2,1,0:T(8,128)}, f32[16,128,128]{2,1,0:T(8,128)}, u32[]{:S(2)}, u32[]{:S(2)}) collective-permute-start(f32[16,128,128]{2,1,0:T(8,128)} %multiply_add_fusion.4), channel_id=1, source_target_pairs={{0,8},{2,10},{4,12},{6,14},{1,9},{3,11},{5,13},{7,15},{16,24},{18,... | collective-permute-start | bytes 3145736 | tf_op jit(solution)/shard_map/ppermute | solution.py:13
  285.7 1.5 fusion.91
  287.2 2.0 copy.200
  289.3 1.5 convolution_bitcast_fusion.3
  290.8 36.1 %collective-permute-done.19 = f32[16,128,128]{2,1,0:T(8,128)} collective-permute-done((f32[16,128,128]{2,1,0:T(8,128)}, f32[16,128,128]{2,1,0:T(8,128)}, u32[]{:S(2)}, u32[]{:S(2)}) %collective-permute-start.19) | collective-permute-done | bytes 1048608 | tf_op jit(solution)/shard_map/ppermute | solution.py:13
  326.9 1.7 multiply_add_fusion
  328.6 1.4 collective-permute-start.20
  330.1 1.7 multiply_add_fusion.3
  331.8 3.2 collective-permute-start.16
  335.0 1.3 convolution_bitcast_fusion
  336.8 1.7 fusion.90
  338.5 2.1 copy.201
  340.6 1.7 fusion.2
  342.4 1.5 fusion.89
  343.9 2.0 copy.202
  346.8 1.3 collective-permute-start.21
  348.1 2.5 copy.157
  350.6 2.5 copy.170
  353.2 2.6 copy.203
  355.8 4.3 multiply_reduce_fusion.11
  360.1 1.7 multiply_reduce_fusion.7
  361.9 1.7 multiply_reduce_fusion.3
  365.5 29.9 %all_to_all.19 = bf16[128,16,128]{0,2,1:T(8,128)(2,1)S(1)} all-to-all(bf16[128,16,128]{0,2,1:T(8,128)(2,1)S(1)} %bitcast.200), channel_id=1, replica_groups=mesh['parts'=2,'seq'=8,'rep'=2,'head'=1] {'seq','rep'}, dimensions={1} | all-to-all | bytes 1048576 | tf_op jit(solution)/shard_map/all_to_all | solution.py:263
  396.7 7.3 %fusion.1 = bf16[1,128,2048]{2,1,0:T(8,128)(2,1)} fusion(bf16[128,2048]{1,0:T(8,128)(2,1)S(1)} %copy-done.10, bf16[2048,2048]{1,0:T(8,128)(2,1)} %all-gather.4.cloned.1.call-done), kind=kOutput, calls=%fused_computation.4 | convolution fusion | flops 1074003968 | bytes 9437184 | tf_op jit(solution)/shard_map/dot_general | solution.py:254
  404.0 10.0 %all-gather.8.cloned.1.call-done = f32[16,3,4,2048]{3,2,1,0:T(4,128)} async-done(((f32[1,3,4,2048]{3,2,1,0:T(4,128)}), f32[16,3,4,2048]{3,2,1,0:T(4,128)}) %all-gather.8.cloned.1.call-update) | async-done | bytes 1572880 | tf_op jit(solution)/shard_map/all_gather | solution.py:253
  414.0 2.4 reduce_sum.149
  416.3 73.5 %all-gather.6.cloned.1.call-done = bf16[2048,2048]{1,0:T(8,128)(2,1)} async-done(((bf16[128,2048]{1,0:T(8,128)(2,1)}), bf16[2048,2048]{1,0:T(8,128)(2,1)}) %all-gather.6.cloned.1.call-update) | async-done | bytes 8388624 | tf_op jit(solution)/shard_map/all_gather | solution.py:264
  489.8 5.8 %fusion = f32[128,2048]{0,1:T(8,128)S(1)} fusion(bf16[2048,2048]{1,0:T(8,128)(2,1)} %all-gather.6.cloned.1.call-done, bf16[2048,128]{1,0:T(8,128)(2,1)S(1)} %bitcast.204), kind=kOutput, calls=%fused_computation.1 | convolution fusion | flops 1074003968 | bytes 9961472 | tf_op jit(solution)/shard_map/dot_general | solution.py:266
  495.6 1.3 copy.184
  (119 shorter events, 25.2 us)
Async XLA Ops:
  7.2 80.1 %copy-start.14 = (bf16[1,128,2048]{2,1,0:T(8,128)(2,1)S(1)}, bf16[1,128,2048]{2,1,0:T(8,128)(2,1)}, u32[]{:S(2)}) copy-start(bf16[1,128,2048]{2,1,0:T(8,128)(2,1)} %param.7) | copy-start | bytes 1572868
  7.2 80.1 %all-gather.4.cloned.1.call-start = ((), (), s32[]{:S(2)}) async-start(), calls=%async_computation.1 | async-start | bytes 8912896 | tf_op jit(solution)/shard_map/all_gather | solution.py:118
  7.9 406.1 %all-gather.8.cloned.1.call-start = ((), (), s32[]{:S(2)}) async-start(), calls=%async_computation.3 | async-start | bytes 1671168 | tf_op jit(solution)/shard_map/all_gather | solution.py:253
  11.8 83.2 %copy-start.24 = (bf16[1,128,2048]{2,1,0:T(8,128)(2,1)S(1)}, bf16[1,128,2048]{2,1,0:T(8,128)(2,1)}, u32[]{:S(2)}) copy-start(bf16[1,128,2048]{2,1,0:T(8,128)(2,1)} %param.10) | copy-start | bytes 1572868
  11.8 83.2 %copy-start.25 = (bf16[1,128,2048]{2,1,0:T(8,128)(2,1)S(1)}, bf16[1,128,2048]{2,1,0:T(8,128)(2,1)}, u32[]{:S(2)}) copy-start(bf16[1,128,2048]{2,1,0:T(8,128)(2,1)} %param.9) | copy-start | bytes 1572868
  91.9 3.1 copy-start.16
  92.0 3.0 collective-permute-start.2
  98.0 1.0 copy-start.3
  98.5 4.5 copy-start
  99.4 5.6 %collective-permute-start.3 = (f32[16,128,128]{2,1,0:T(8,128)S(1)}, f32[16,128,128]{2,1,0:T(8,128)S(1)}, u32[]{:S(2)}, u32[]{:S(2)}) collective-permute-start(f32[16,128,128]{2,1,0:T(8,128)S(1)} %fusion.57), channel_id=1, source_target_pairs={{0,2},{2,4},{4,6},{6,8},{8,10},{10,12},{12,14},{1,3},{3,5},{5,7},{... | collective-permute-start | bytes 3145736 | tf_op jit(solution)/shard_map/ppermute | solution.py:13
  103.1 6.3 %collective-permute-start.9 = (f32[16,128,128]{2,1,0:T(8,128)S(1)}, f32[16,128,128]{2,1,0:T(8,128)S(1)}, u32[]{:S(2)}, u32[]{:S(2)}) collective-permute-start(f32[16,128,128]{2,1,0:T(8,128)S(1)} %fusion.55), channel_id=1, source_target_pairs={{2,0},{4,2},{6,4},{8,6},{10,8},{12,10},{14,12},{3,1},{5,3},{7,5},{... | collective-permute-start | bytes 3145736 | tf_op jit(solution)/shard_map/ppermute | solution.py:13
  109.9 36.4 %collective-permute-start.10 = (f32[16,128,128]{2,1,0:T(8,128)S(1)}, f32[16,128,128]{2,1,0:T(8,128)S(1)}, u32[]{:S(2)}, u32[]{:S(2)}) collective-permute-start(f32[16,128,128]{2,1,0:T(8,128)S(1)} %get-tuple-element.72), channel_id=1, source_target_pairs={{4,0},{6,2},{8,4},{10,6},{12,8},{14,10},{5,1},{7,3},{9,5},{11,7},{... | collective-permute-start | bytes 3145736 | tf_op jit(solution)/shard_map/ppermute | solution.py:13
  111.2 37.6 %collective-permute-start.4 = (f32[16,128,128]{2,1,0:T(8,128)S(1)}, f32[16,128,128]{2,1,0:T(8,128)S(1)}, u32[]{:S(2)}, u32[]{:S(2)}) collective-permute-start(f32[16,128,128]{2,1,0:T(8,128)S(1)} %get-tuple-element.71), channel_id=1, source_target_pairs={{0,4},{2,6},{4,8},{6,10},{8,12},{10,14},{1,5},{3,7},{5,9},{7,11},{... | collective-permute-start | bytes 3145736 | tf_op jit(solution)/shard_map/ppermute | solution.py:13
  125.6 4.9 collective-permute-start
  129.3 3.1 collective-permute-start.7
  147.5 53.6 %collective-permute-start.11 = (f32[16,128,128]{2,1,0:T(8,128)}, f32[16,128,128]{2,1,0:T(8,128)}, u32[]{:S(2)}, u32[]{:S(2)}) collective-permute-start(f32[16,128,128]{2,1,0:T(8,128)} %multiply_add_fusion.7), channel_id=1, source_target_pairs={{8,0},{10,2},{12,4},{14,6},{9,1},{11,3},{13,5},{15,7},{24,16},{26,... | collective-permute-start | bytes 3145736 | tf_op jit(solution)/shard_map/ppermute | solution.py:13
  150.0 54.3 %collective-permute-start.5 = (f32[16,128,128]{2,1,0:T(8,128)}, f32[16,128,128]{2,1,0:T(8,128)}, u32[]{:S(2)}, u32[]{:S(2)}) collective-permute-start(f32[16,128,128]{2,1,0:T(8,128)} %multiply_add_fusion.10), channel_id=1, source_target_pairs={{0,8},{2,10},{4,12},{6,14},{1,9},{3,11},{5,13},{7,15},{16,24},{18,... | collective-permute-start | bytes 3145736 | tf_op jit(solution)/shard_map/ppermute | solution.py:13
  162.8 19.2 %collective-permute-start.1 = (f32[16]{0:T(128)S(1)}, f32[16]{0:T(128)S(1)}, u32[]{:S(2)}, u32[]{:S(2)}) collective-permute-start(f32[16]{0:T(128)S(1)} %get-tuple-element.69), channel_id=1, source_target_pairs={{0,4},{2,6},{4,8},{6,10},{8,12},{10,14},{1,5},{3,7},{5,9},{7,11},{... | collective-permute-start | bytes 200 | tf_op jit(solution)/shard_map/ppermute | solution.py:13
  166.8 15.2 %collective-permute-start.8 = (f32[16]{0:T(128)S(1)}, f32[16]{0:T(128)S(1)}, u32[]{:S(2)}, u32[]{:S(2)}) collective-permute-start(f32[16]{0:T(128)S(1)} %get-tuple-element.70), channel_id=1, source_target_pairs={{4,0},{6,2},{8,4},{10,6},{12,8},{14,10},{5,1},{7,3},{9,5},{11,7},{... | collective-permute-start | bytes 200 | tf_op jit(solution)/shard_map/ppermute | solution.py:13
  187.1 22.2 %copy-start.20 = (bf16[16,128,128]{2,1,0:T(8,128)(2,1)}, bf16[16,128,128]{2,1,0:T(8,128)(2,1)S(1)}, u32[]{:S(2)}) copy-start(bf16[16,128,128]{2,1,0:T(8,128)(2,1)S(1)} %fusion.18) | copy-start | bytes 1572868
  202.9 6.4 %copy-start.1 = (bf16[16,16,8,128]{3,2,1,0:T(8,128)(2,1)S(1)}, bf16[16,16,8,128]{3,2,1,0:T(8,128)(2,1)}, u32[]{:S(2)}) copy-start(bf16[16,16,8,128]{3,2,1,0:T(8,128)(2,1)} %copy-done) | copy-start | bytes 1572868
  202.9 6.9 %collective-permute-start.12 = (bf16[16,128,128]{2,1,0:T(8,128)(2,1)S(1)}, bf16[16,128,128]{2,1,0:T(8,128)(2,1)S(1)}, u32[]{:S(2)}, u32[]{:S(2)}) collective-permute-start(bf16[16,128,128]{2,1,0:T(8,128)(2,1)S(1)} %multiply_add_fusion.6), channel_id=1, source_target_pairs={{2,0},{4,2},{6,4},{8,6},{10,8},{12,10},{14,12},{3,1},{5,3},{7,5},{... | collective-permute-start | bytes 1572872 | tf_op jit(solution)/shard_map/ppermute | solution.py:13
  206.1 3.8 copy-start.8
  206.1 4.7 collective-permute-start.6
  210.2 1.2 copy-start.9
  212.6 73.1 %copy-start.6 = (bf16[128,16,128]{0,2,1:T(8,128)(2,1)}, bf16[128,16,128]{0,2,1:T(8,128)(2,1)S(1)}, u32[]{:S(2)}) copy-start(bf16[128,16,128]{0,2,1:T(8,128)(2,1)S(1)} %get-tuple-element.42) | copy-start | bytes 1572868
  213.6 18.2 %collective-permute-start.13 = (f32[16,128,128]{2,1,0:T(8,128)S(1)}, f32[16,128,128]{2,1,0:T(8,128)S(1)}, u32[]{:S(2)}, u32[]{:S(2)}) collective-permute-start(f32[16,128,128]{2,1,0:T(8,128)S(1)} %fusion.53), channel_id=1, source_target_pairs={{0,2},{2,4},{4,6},{6,8},{8,10},{10,12},{12,14},{1,3},{3,5},{5,7},{... | collective-permute-start | bytes 3145736 | tf_op jit(solution)/shard_map/ppermute | solution.py:13
  229.6 6.5 %collective-permute-start.17 = (f32[16,128,128]{2,1,0:T(8,128)S(1)}, f32[16,128,128]{2,1,0:T(8,128)S(1)}, u32[]{:S(2)}, u32[]{:S(2)}) collective-permute-start(f32[16,128,128]{2,1,0:T(8,128)S(1)} %fusion.51), channel_id=1, source_target_pairs={{2,0},{4,2},{6,4},{8,6},{10,8},{12,10},{14,12},{3,1},{5,3},{7,5},{... | collective-permute-start | bytes 3145736 | tf_op jit(solution)/shard_map/ppermute | solution.py:13
  236.7 35.7 %collective-permute-start.18 = (f32[16,128,128]{2,1,0:T(8,128)S(1)}, f32[16,128,128]{2,1,0:T(8,128)S(1)}, u32[]{:S(2)}, u32[]{:S(2)}) collective-permute-start(f32[16,128,128]{2,1,0:T(8,128)S(1)} %get-tuple-element.68), channel_id=1, source_target_pairs={{4,0},{6,2},{8,4},{10,6},{12,8},{14,10},{5,1},{7,3},{9,5},{11,7},{... | collective-permute-start | bytes 3145736 | tf_op jit(solution)/shard_map/ppermute | solution.py:13
  238.0 37.1 %collective-permute-start.14 = (f32[16,128,128]{2,1,0:T(8,128)S(1)}, f32[16,128,128]{2,1,0:T(8,128)S(1)}, u32[]{:S(2)}, u32[]{:S(2)}) collective-permute-start(f32[16,128,128]{2,1,0:T(8,128)S(1)} %get-tuple-element.67), channel_id=1, source_target_pairs={{0,4},{2,6},{4,8},{6,10},{8,12},{10,14},{1,5},{3,7},{5,9},{7,11},{... | collective-permute-start | bytes 3145736 | tf_op jit(solution)/shard_map/ppermute | solution.py:13
  253.1 32.1 %copy-start.22 = (bf16[16,128,128]{2,1,0:T(8,128)(2,1)}, bf16[16,128,128]{2,1,0:T(8,128)(2,1)S(1)}, u32[]{:S(2)}) copy-start(bf16[16,128,128]{2,1,0:T(8,128)(2,1)S(1)} %fusion.19) | copy-start | bytes 1572868
  273.6 11.6 %copy-start.4 = (bf16[128,2048]{0,1:T(8,128)(2,1)S(1)}, bf16[128,2048]{0,1:T(8,128)(2,1)}, u32[]{:S(2)}) copy-start(bf16[128,2048]{0,1:T(8,128)(2,1)} %copy.141) | copy-start | bytes 1572868
  273.6 53.3 %collective-permute-start.19 = (f32[16,128,128]{2,1,0:T(8,128)}, f32[16,128,128]{2,1,0:T(8,128)}, u32[]{:S(2)}, u32[]{:S(2)}) collective-permute-start(f32[16,128,128]{2,1,0:T(8,128)} %multiply_add_fusion.1), channel_id=1, source_target_pairs={{8,0},{10,2},{12,4},{14,6},{9,1},{11,3},{13,5},{15,7},{24,16},{26,... | collective-permute-start | bytes 3145736 | tf_op jit(solution)/shard_map/ppermute | solution.py:13
  276.2 53.9 %collective-permute-start.15 = (f32[16,128,128]{2,1,0:T(8,128)}, f32[16,128,128]{2,1,0:T(8,128)}, u32[]{:S(2)}, u32[]{:S(2)}) collective-permute-start(f32[16,128,128]{2,1,0:T(8,128)} %multiply_add_fusion.4), channel_id=1, source_target_pairs={{0,8},{2,10},{4,12},{6,14},{1,9},{3,11},{5,13},{7,15},{16,24},{18,... | collective-permute-start | bytes 3145736 | tf_op jit(solution)/shard_map/ppermute | solution.py:13
  328.6 6.4 %copy-start.7 = (bf16[128,16,128]{0,2,1:T(8,128)(2,1)S(1)}, bf16[128,16,128]{0,2,1:T(8,128)(2,1)}, u32[]{:S(2)}) copy-start(bf16[128,16,128]{0,2,1:T(8,128)(2,1)} %copy-done.6) | copy-start | bytes 1572868
  328.6 6.4 %copy-start.21 = (bf16[16,128,128]{2,1,0:T(8,128)(2,1)S(1)}, bf16[16,128,128]{2,1,0:T(8,128)(2,1)}, u32[]{:S(2)}) copy-start(bf16[16,128,128]{2,1,0:T(8,128)(2,1)} %copy-done.20) | copy-start | bytes 1572868
  328.6 7.7 %collective-permute-start.20 = (bf16[16,128,128]{2,1,0:T(8,128)(2,1)S(1)}, bf16[16,128,128]{2,1,0:T(8,128)(2,1)S(1)}, u32[]{:S(2)}, u32[]{:S(2)}) collective-permute-start(bf16[16,128,128]{2,1,0:T(8,128)(2,1)S(1)} %multiply_add_fusion), channel_id=1, source_target_pairs={{2,0},{4,2},{6,4},{8,6},{10,8},{12,10},{14,12},{3,1},{5,3},{7,5},{... | collective-permute-start | bytes 1572872 | tf_op jit(solution)/shard_map/ppermute | solution.py:13
  331.8 4.5 copy-start.2
  331.8 5.0 collective-permute-start.16
  336.3 2.2 copy-start.23
  336.8 1.7 copy-start.17
  340.6 1.7 copy-start.5
  340.6 1.7 copy-start.13
  340.6 1.8 copy-start.18
  346.8 9.0 %collective-permute-start.21 = (bf16[3,3,2048]{2,1,0:T(4,128)(2,1)S(1)}, bf16[3,3,2048]{2,1,0:T(4,128)(2,1)S(1)}, u32[]{:S(2)}, u32[]{:S(2)}) collective-permute-start(bf16[3,3,2048]{2,1,0:T(4,128)(2,1)S(1)} %pad_maximum_fusion.3), channel_id=1, source_target_pairs={{2,0},{4,2},{6,4},{8,6},{10,8},{12,10},{14,12},{3,1},{5,3},{7,5},{... | collective-permute-start | bytes 110600 | tf_op jit(solution)/shard_map/ppermute | solution.py:13
  355.8 4.3 copy-start.12
  360.1 1.7 copy-start.11
  363.6 1.6 copy-start.15
  364.4 125.4 %all-gather.6.cloned.1.call-start = ((), (), s32[]{:S(2)}) async-start(), calls=%async_computation.2 | async-start | bytes 8912896 | tf_op jit(solution)/shard_map/all_gather | solution.py:264
  365.4 30.2 %copy-start.19 = (bf16[128,16,128]{0,2,1:T(8,128)(2,1)S(1)}, bf16[128,16,128]{0,2,1:T(8,128)(2,1)}, u32[]{:S(2)}) copy-start(bf16[128,16,128]{0,2,1:T(8,128)(2,1)} %get-tuple-element.43) | copy-start | bytes 1572868
  395.4 1.3 copy-start.10
Sparse Core Ops, SparseCore 0:
  10.2 76.9 all-gather.3
  364.5 49.3 all-gather.7
  416.8 72.9 all-gather.5
